TPU v7x, 256 devices: a whole 4x4x8 slice. The times are simulated.
256 devices in a mesh: lat: 64 (over x, y_lo, z), dp: 4 (over y_hi, core).
Axes of the slice: x: 4, y: 4 (y_hi: 2, y_lo: 2; y = y_hi * 2 + y_lo), z: 8, core: 2. Of those that a mesh axis runs over, the one named last changes fastest.
Arguments:
- inputs: bfloat16 [2048, 4096], P('dp', 'lat'), may hold values from -6 to 6
- dec_bias: bfloat16 [4096], P('lat'), may hold values from -3 to 3
- enc_weight: bfloat16 [4096, 16384], P(None, 'lat'), may hold values from -0.09375 to 0.09375
- enc_bias: float32 [16384], P('lat'), may hold values from -3 to 3
- dec_weight: bfloat16 [16384, 4096], P('lat'), may hold values from -0.046875 to 0.046875
- other_recon: float32 [2048, 4096], P('dp', 'lat'), may hold values from -6 to 6
- active_blocks: int32 [2048, 128], P('dp', 'lat'), may hold values 0 or 1
Outputs:
- error_full: float32 [2048, 4096], P('dp', 'lat')
- mse_loss: float32 [], replicated
- grad_dec: float32 [16384, 4096], P(('lat', 'dp'))
- grad_enc: float32 [4096, 16384], P(None, ('lat', 'dp'))
All inputs are finite; a program needn't handle non-finite values. No bound on the sum of `active_blocks` on one device may be relied on, other than what follows from the above.
Results may differ from a plain program's by a relative error of at most 0.0033.
Values may be sent and summed in bfloat16 or wider, within the bound.
A program may use at most 128 MiB of HBM per device.

v0:
```python
import jax
import jax.numpy as jnp
from jax import lax
from jax.sharding import PartitionSpec as P


def local(inputs, dec_bias, enc_weight, enc_bias, dec_weight, other_recon, active_blocks):
    row_count = inputs.shape[0]
    col_count = inputs.shape[1]
    block_size = enc_weight.shape[1] // active_blocks.shape[1]
    full_inputs, full_bias = (
        lax.all_gather(inputs, "lat", axis=1, tiled=True),
        lax.all_gather(dec_bias.reshape(1, -1), "lat", axis=1, tiled=True),
    )
    inputs_float = full_inputs.astype(jnp.float32)
    centered = (inputs_float - full_bias.astype(jnp.float32)).astype(jnp.bfloat16)
    pre_act = jnp.dot(centered, enc_weight, preferred_element_type=jnp.float32) + enc_bias[None, :]
    block_gate = (
        active_blocks.astype(jnp.float32)[:, :, None] * jnp.ones((1, 1, block_size), jnp.float32)
    ).reshape(row_count, -1)
    positive = jnp.maximum(pre_act, 0.0)
    activations = (positive * positive * block_gate).astype(jnp.bfloat16)
    outside = other_recon + dec_bias.astype(jnp.float32)[None, :]
    summed = lax.psum_scatter(
        lax.dot_general(
            dec_weight, activations, (((0,), (1,)), ((), ())), preferred_element_type=jnp.float32
        ),
        "lat",
        scatter_dimension=0,
        tiled=True,
    )
    error_local = summed.T + outside - inputs.astype(jnp.float32)
    error_bf = lax.all_gather(error_local.astype(jnp.bfloat16), "lat", axis=1, tiled=True)
    squares = lax.psum(jnp.sum(error_local * error_local), ("lat", "dp"))
    mse_loss = squares / (row_count * lax.axis_size("dp") * col_count * lax.axis_size("lat"))
    grad_dec = lax.psum_scatter(
        lax.dot_general(
            activations, error_bf, (((0,), (0,)), ((), ())), preferred_element_type=jnp.float32
        ),
        "dp",
        scatter_dimension=0,
        tiled=True,
    )
    dact = lax.dot_general(
        error_bf, dec_weight, (((1,), (1,)), ((), ())), preferred_element_type=jnp.float32
    )
    dpre = (dact * 2.0 * positive * block_gate).astype(jnp.bfloat16)
    enc_term = lax.dot_general(
        centered, dpre, (((0,), (0,)), ((), ())), preferred_element_type=jnp.float32
    )
    grad_enc = lax.psum_scatter(enc_term, "dp", scatter_dimension=1, tiled=True)
    return (error_local, mse_loss, grad_dec, grad_enc)


def solution(mesh):
    placed = (
        P("dp", "lat"),
        P("lat"),
        P(None, "lat"),
        P("lat"),
        P("lat", None),
        P("dp", "lat"),
        P("dp", "lat"),
    )
    return jax.shard_map(
        local,
        mesh=mesh,
        in_specs=placed,
        out_specs=(P("dp", "lat"), P(), P(("lat", "dp"), None), P(None, ("lat", "dp"))),
        check_vma=False,
    )
```

profile of v0, /device:TPU:1, one launch (start us, length us, event | category | flops | bytes accessed | tf_op | source)
XLA Modules:
  0.0 1096.9 jit_solution(8180831337322198771)
XLA Ops:
  7.2 0.0 all-gather.4.cloned.1.call-start
  7.2 0.7 all-gather.4.cloned.1.call-update
  7.9 0.0 reduce-scatter.10.cloned.1.call-start
  8.0 0.7 convert_element_type.27
  8.7 0.1 copy.15
  8.8 1.3 dynamic-slice
  10.8 0.9 dynamic-update-slice
  11.6 139.7 %all-reduce = bf16[4096]{0:T(1024)(128)(2,1)S(1)} all-reduce(bf16[4096]{0:T(1024)(128)(2,1)S(1)} %dynamic-update-slice), channel_id=2, replica_groups=mesh['lat'=64,'dp'=4] {'lat'}, use_global_device_ids=true, to_apply=%add | all-reduce | flops 4096 | bytes 16384
  151.4 123.1 %all-gather.4.cloned.1.call-done = bf16[512,4096]{0,1:T(8,128)(2,1)} async-done(((bf16[512,64]{0,1:T(8,128)(2,1)}), bf16[512,4096]{0,1:T(8,128)(2,1)}) %all-gather.4.cloned.1.call-update) | async-done | bytes 4194320 | tf_op jit(solution)/shard_map/all_gather | solution.py:12
  274.5 0.6 mul.27
  275.1 5.8 fusion.8
  280.8 4.5 convolution_bitcast_fusion
  285.3 9.0 copy.20
  294.3 0.0 reduce-scatter.10.cloned.1.call-update
  294.4 0.0 all-gather.6.cloned.1.call-start
  294.4 0.8 copy-done.2
  295.2 0.1 copy.17
  295.3 0.1 copy.16
  295.5 324.6 %reduce-scatter.10.cloned.1.call-done = f32[64,512]{1,0:T(8,128)} async-done(((f32[4096,512]{1,0:T(8,128)}), f32[64,512]{1,0:T(8,128)}) %reduce-scatter.10.cloned.1.call-update) | async-done | bytes 131088
  620.1 1.0 copy.21
  621.2 0.7 copy.18
  621.9 0.0 all-gather.6.cloned.1.call-update
  621.9 0.0 reduce-scatter.8.cloned.1.call-start
  622.0 300.7 %all-gather.6.cloned.1.call-done = bf16[512,4096]{0,1:T(8,128)(2,1)} async-done(((bf16[512,64]{0,1:T(8,128)(2,1)}), bf16[512,4096]{0,1:T(8,128)(2,1)}) %all-gather.6.cloned.1.call-update) | async-done | bytes 4194320 | tf_op jit(solution)/shard_map/all_gather | solution.py:33
  922.7 10.2 fusion
  932.9 0.0 reduce-scatter.6.cloned.1.call-start
  933.0 5.4 fusion.15
  938.5 0.7 multiply_reduce_fusion
  939.1 117.6 %psum.7 = f32[]{:T(128)} all-reduce(f32[]{:T(128)} %multiply_reduce_fusion), channel_id=1, replica_groups=mesh['lat'=64,'dp'=4] {'lat','dp'}, use_global_device_ids=true, to_apply=%region_2.0 | all-reduce | flops 1 | bytes 8 | tf_op jit(solution)/shard_map/psum | solution.py:34
  1056.8 0.8 copy.19
  1058.2 0.0 reduce-scatter.8.cloned.1.call-done
  1058.2 31.0 %reduce-scatter.6.cloned.1.call-done = f32[64,4096]{1,0:T(8,128)} async-done(((f32[256,4096]{1,0:T(8,128)}), f32[64,4096]{1,0:T(8,128)}) %reduce-scatter.6.cloned.1.call-update) | async-done | bytes 1048592 | tf_op jit(solution)/shard_map/reduce_scatter | solution.py:36
  (15 shorter events, 0.1 us)
Async XLA Ops:
  7.2 273.7 %copy-start = (bf16[256,4096]{1,0:T(8,128)(2,1)S(1)}, bf16[256,4096]{1,0:T(8,128)(2,1)}, u32[]{:S(2)}) copy-start(bf16[256,4096]{1,0:T(8,128)(2,1)} %param.11) | copy-start | bytes 6291460
  7.2 267.3 %all-gather.4.cloned.1.call-start = ((), (), s32[]{:S(2)}) async-start(), calls=%async_computation.3 | async-start | bytes 4259840 | tf_op jit(solution)/shard_map/all_gather | solution.py:12
  7.9 612.2 %reduce-scatter.10.cloned.1.call-start = ((), (), s32[]{:S(2)}) async-start(), calls=%async_computation.7 | async-start | bytes 8519680
  275.1 5.8 copy-start.1
  294.3 0.8 copy-start.2
  294.3 1.0 copy-start.4
  294.3 1.0 copy-start.3
  294.4 628.3 %all-gather.6.cloned.1.call-start = ((), (), s32[]{:S(2)}) async-start(), calls=%async_computation.4 | async-start | bytes 4259840 | tf_op jit(solution)/shard_map/all_gather | solution.py:33
  621.9 436.3 %reduce-scatter.8.cloned.1.call-start = ((), (), s32[]{:S(2)}) async-start(), calls=%async_computation.6 | async-start | bytes 5242880 | tf_op jit(solution)/shard_map/reduce_scatter | solution.py:51
  932.9 156.3 %reduce-scatter.6.cloned.1.call-start = ((), (), s32[]{:S(2)}) async-start(), calls=%async_computation.5 | async-start | bytes 5242880 | tf_op jit(solution)/shard_map/reduce_scatter | solution.py:36
Sparse Core Ops, SparseCore 0:
  9.8 264.6 all-gather.3
  294.5 325.5 reduce-scatter.9
  622.4 300.1 all-gather.5
  933.1 96.8 reduce-scatter.7
  1033.4 55.7 reduce-scatter.5
where the time goes:
time: 1100 us
  waiting for transfers between devices  780 us (71%)
  blocking collectives  257 us (23%)
  matrix products  25.9 us (2%)
  between operations  16.3 us (1%)
  local copies, waits for them, and re-layouts  15.4 us (1%)
    unnamed x6, waiting for transfers between devices  325 us
    all_gather x1, waiting for transfers between devices, local(): lax.all_gather(error_local.astype(jnp.bfloat16), 'lat', axis=1, tiled=True)  301 us
    unnamed x1, blocking collectives  140 us
    all_gather x1, waiting for transfers between devices, local(): lax.all_gather(inputs, 'lat', axis=1, tiled=True)  123 us
    psum x1, blocking collectives, local(): squares = lax.psum(jnp.sum(error_local * error_local), ('lat', 'dp'))  118 us
    reduce_scatter x1, waiting for transfers between devices, local(): lax.psum_scatter(lax.dot_general(activations, error_bf, (((0,), (0,)), ((...  31 us
  transfers between devices with their start and end apart: 5, of which 4 were waited for; matrix products, arithmetic and copies ran while one was open for 1% of the time, Pallas kernels for 0%

commit v1 on v0

--- a/solution.py
+++ b/solution.py
@@ -2,6 +2,13 @@
 import jax.numpy as jnp
 from jax import lax
 from jax.sharding import PartitionSpec as P
+
+
+def exchange_gather(value, mesh_axis, along):
+    size = lax.axis_size(mesh_axis)
+    blocks = jnp.stack([value for _ in range(size)])
+    blocks = lax.all_to_all(blocks, mesh_axis, split_axis=0, concat_axis=0)
+    return jnp.concatenate(blocks, axis=along)
 
 
 def local(inputs, dec_bias, enc_weight, enc_bias, dec_weight, other_recon, active_blocks):
@@ -30,7 +37,7 @@
         tiled=True,
     )
     error_local = summed.T + outside - inputs.astype(jnp.float32)
-    error_bf = lax.all_gather(error_local.astype(jnp.bfloat16), "lat", axis=1, tiled=True)
+    error_bf = exchange_gather(error_local.astype(jnp.bfloat16), "lat", 1)
     squares = lax.psum(jnp.sum(error_local * error_local), ("lat", "dp"))
     mse_loss = squares / (row_count * lax.axis_size("dp") * col_count * lax.axis_size("lat"))
     grad_dec = lax.psum_scatter(

time: 1100 us -> 868 us (0.79)
  waiting for transfers between devices: 780 us -> 479 us
  blocking collectives: 257 us -> 330 us
    all_gather x1 -> x0, waiting for transfers between devices: 301 us -> none  [local(): lax.all_gather(error_local.astype(jnp.bfloat16), 'lat', axis=1, tiled=True)]
    all_to_all x0 -> x1, blocking collectives: none -> 57.4 us  [exchange_gather(): blocks = lax.all_to_all(blocks, mesh_axis, split_axis=0, concat_axis=0)]
    psum x1, blocking collectives: 118 us -> 133 us  [local(): squares = lax.psum(jnp.sum(error_local * error_local), ('lat', 'dp'))]
    unnamed x6 -> x5, waiting for transfers between devices: 325 us -> 325 us
  transfers between devices with their start and end apart: 5 -> 4, of which waited for: 4 -> 3; matrix products, arithmetic and copies ran while one was open for 1% -> 1% of each run, Pallas kernels for 0% -> 0%
where the time goes in v1:
time: 868 us
  waiting for transfers between devices  479 us (55%)
  blocking collectives  330 us (38%)
  matrix products  25.8 us (3%)
  between operations  16.3 us (2%)
  local copies, waits for them, and re-layouts  15.3 us (2%)
    unnamed x5, waiting for transfers between devices  325 us
    unnamed x1, blocking collectives  140 us
    psum x1, blocking collectives, local(): squares = lax.psum(jnp.sum(error_local * error_local), ('lat', 'dp'))  133 us
    all_gather x1, waiting for transfers between devices, local(): lax.all_gather(inputs, 'lat', axis=1, tiled=True)  123 us
    all_to_all x1, blocking collectives, exchange_gather(): blocks = lax.all_to_all(blocks, mesh_axis, split_axis=0, concat_axis=0)  57.4 us
    reduce_scatter x1, waiting for transfers between devices, local(): lax.psum_scatter(lax.dot_general(activations, error_bf, (((0,), (0,)), ((...  30.5 us
  transfers between devices with their start and end apart: 4, of which 3 were waited for; matrix products, arithmetic and copies ran while one was open for 1% of the time, Pallas kernels for 0%

profile of v1, /device:TPU:1, one launch (start us, length us, event | category | flops | bytes accessed | tf_op | source)
XLA Modules:
  0.0 867.7 jit_solution(4835640428335427953)
XLA Ops:
  7.2 0.0 all-gather.3.cloned.1.call-start
  7.2 0.7 all-gather.3.cloned.1.call-update
  7.9 0.0 reduce-scatter.10.cloned.1.call-start
  8.0 0.7 convert_element_type.27
  8.7 0.1 copy.20
  8.8 1.3 dynamic-slice
  10.8 0.9 dynamic-update-slice
  11.6 139.7 %all-reduce = bf16[4096]{0:T(1024)(128)(2,1)S(1)} all-reduce(bf16[4096]{0:T(1024)(128)(2,1)S(1)} %dynamic-update-slice), channel_id=2, replica_groups=mesh['lat'=64,'dp'=4] {'lat'}, use_global_device_ids=true, to_apply=%add | all-reduce | flops 4096 | bytes 16384
  151.4 123.1 %all-gather.3.cloned.1.call-done = bf16[512,4096]{0,1:T(8,128)(2,1)} async-done(((bf16[512,64]{0,1:T(8,128)(2,1)}), bf16[512,4096]{0,1:T(8,128)(2,1)}) %all-gather.3.cloned.1.call-update) | async-done | bytes 4194320 | tf_op jit(solution)/shard_map/all_gather | solution.py:19
  274.5 0.6 mul.27
  275.1 5.8 fusion.8
  280.8 4.5 convolution_bitcast_fusion
  285.3 9.0 %copy.25 = f32[4096,512]{1,0:T(8,128)} copy(f32[4096,512]{0,1:T(8,128)} %convolution_bitcast_fusion) | data formatting | bytes 16777216
  294.4 0.0 reduce-scatter.10.cloned.1.call-update
  294.4 0.0 reduce-scatter.8.cloned.1.call-start
  294.4 0.8 copy-done.3
  295.2 0.1 copy.22
  295.4 0.1 copy.21
  295.5 324.6 %reduce-scatter.10.cloned.1.call-done = f32[64,512]{1,0:T(8,128)} async-done(((f32[4096,512]{1,0:T(8,128)}), f32[64,512]{1,0:T(8,128)}) %reduce-scatter.10.cloned.1.call-update) | async-done | bytes 131088
  620.1 1.0 copy.26
  621.1 0.1 fusion.13
  621.2 0.1 copy.23
  621.3 0.5 stack.2
  621.8 57.4 %all_to_all.5 = bf16[64,512,64]{1,2,0:T(8,128)(2,1)} all-to-all(bf16[64,512,64]{1,2,0:T(8,128)(2,1)S(1)} %stack.2), channel_id=1, replica_groups=mesh['lat'=64,'dp'=4] {'lat'}, dimensions={0} | all-to-all | bytes 8388608 | tf_op jit(solution)/shard_map/all_to_all | solution.py:10
  679.2 10.1 %fusion = f32[4096,256]{0,1:T(8,128)} fusion(bf16[512,4096]{0,1:T(8,128)(2,1)} %all-gather.3.cloned.1.call-done, f32[4096]{0:T(1024)S(1)} %sub.22, f32[512,256]{1,0:T(8,128)} %get-tuple-element.19, bf16[512,4096]{0,1:T(8,128)(2,1)} %bitcast.28, bf16[256,4096]{1,0:T(8,128)(2,1)S(1)} %copy-done, f32[64,8,2,128]{3,2,1,0:T(2,128)S(1)} %bitcast.31), kind=kOutput, calls=%fused_computation.2 | convolution fusion | flops 2154299392 | bytes 15745024 | tf_op jit(solution)/shard_map/dot_general | solution.py:55
  689.3 0.0 reduce-scatter.6.cloned.1.call-start
  689.4 5.5 fusion.15
  694.8 0.7 multiply_reduce_fusion
  695.5 132.7 %psum.7 = f32[]{:T(128)} all-reduce(f32[]{:T(128)} %multiply_reduce_fusion), channel_id=1, replica_groups=mesh['lat'=64,'dp'=4] {'lat','dp'}, use_global_device_ids=true, to_apply=%region_2.0 | all-reduce | flops 1 | bytes 8 | tf_op jit(solution)/shard_map/psum | solution.py:41
  828.2 0.8 copy.24
  829.6 0.0 reduce-scatter.8.cloned.1.call-done
  829.6 30.5 %reduce-scatter.6.cloned.1.call-done = f32[64,4096]{1,0:T(8,128)} async-done(((f32[256,4096]{1,0:T(8,128)}), f32[64,4096]{1,0:T(8,128)}) %reduce-scatter.6.cloned.1.call-update) | async-done | bytes 1048592 | tf_op jit(solution)/shard_map/reduce_scatter | solution.py:43
  (16 shorter events, 0.1 us)
Async XLA Ops:
  7.2 273.7 %copy-start = (bf16[256,4096]{1,0:T(8,128)(2,1)S(1)}, bf16[256,4096]{1,0:T(8,128)(2,1)}, u32[]{:S(2)}) copy-start(bf16[256,4096]{1,0:T(8,128)(2,1)} %param.11) | copy-start | bytes 6291460
  7.2 267.3 %all-gather.3.cloned.1.call-start = ((), (), s32[]{:S(2)}) async-start(), calls=%async_computation.4 | async-start | bytes 4259840 | tf_op jit(solution)/shard_map/all_gather | solution.py:19
  7.9 612.2 %reduce-scatter.10.cloned.1.call-start = ((), (), s32[]{:S(2)}) async-start(), calls=%async_computation.7 | async-start | bytes 8519680
  275.1 5.8 copy-start.1
  294.4 0.8 copy-start.3
  294.4 1.0 copy-start.5
  294.4 1.0 copy-start.4
  294.4 535.2 %reduce-scatter.8.cloned.1.call-start = ((), (), s32[]{:S(2)}) async-start(), calls=%async_computation.6 | async-start | bytes 5242880 | tf_op jit(solution)/shard_map/reduce_scatter | solution.py:58
  621.8 57.4 %copy-start.2 = (f32[512,2,128]{2,1,0:T(2,128)S(1)}, f32[512,2,128]{2,1,0:T(2,128)}, u32[]{:S(2)}) copy-start(f32[512,2,128]{2,1,0:T(2,128)} %copy-done.1) | copy-start | bytes 1572868
  689.3 170.8 %reduce-scatter.6.cloned.1.call-start = ((), (), s32[]{:S(2)}) async-start(), calls=%async_computation.5 | async-start | bytes 5242880 | tf_op jit(solution)/shard_map/reduce_scatter | solution.py:43
Sparse Core Ops, SparseCore 0:
  9.8 264.6 all-gather.2
  294.5 325.5 reduce-scatter.9
  689.4 111.2 reduce-scatter.7
  804.1 55.9 reduce-scatter.5
